TPU v7x, 32 devices: a whole 2x2x4 slice. The times are simulated.
32 devices in a mesh: band: 8 (over z, x), coef: 4 (over y, core).
Axes of the slice: x: 2, y: 2, z: 4, core: 2. Of those that a mesh axis runs over, the one named last changes fastest.
Arguments:
- coeffs: float32 [1024, 262144], P('band', 'coef'), may hold values from -320 to 320
- ref_block: float32 [1024, 262144], P('band', 'coef'), may hold values from -0.01171875 to 0.01171875
- index_map: int32 [262144], P('coef'), may hold values from 0 to 65535, as said below
- band_group: int32 [1024], P('band'), may hold values from 0 to 15
Outputs:
- ortho: float32 [1024, 262144], P('band', 'coef')
- band_residual: float32 [1024], P('band')
- group_residual: float32 [16], replicated
Inputs may be any that keep to these rules, and one draw needn't show every extreme that they name: Within each aligned slab of 65536 coefficients, index_map holds every number of 0 to 65535 once.
All inputs are finite; a program needn't handle non-finite values.
Results may differ from a plain program's by a relative error of at most 0.000098.
Values sent between devices are 32-bit elements; how exact they have to be, the bound alone decides.
A program may use at most 384 MiB of HBM per device.

v0:
```python
import jax
import jax.numpy as jnp
from jax import lax
from jax.sharding import PartitionSpec as P

NB = 1024
NGROUPS = 16


def local(coeffs, ref_block, index_map, band_group):
    columns = lax.all_to_all(coeffs, "band", split_axis=1, concat_axis=0, tiled=True)
    partial_value = jnp.dot(
        columns, columns.T, precision=lax.Precision.HIGHEST, preferred_element_type=jnp.float32
    )
    margin = lax.psum(partial_value, ("band", "coef"))
    factor = jnp.linalg.cholesky(margin)
    ortho_cols = lax.linalg.triangular_solve(factor, columns, left_side=True, lower=True)
    ortho = lax.all_to_all(ortho_cols, "band", split_axis=0, concat_axis=1, tiled=True)
    aligned = jnp.take(ortho, index_map, axis=1)
    squares = jnp.sum((aligned - ref_block) ** 2, axis=1)
    group_range = jnp.arange(NGROUPS, dtype=jnp.int32)
    totals = lax.psum(squares, "coef")
    band_residual = jnp.sqrt(totals + 1e-06)
    onehot = (band_group[:, None] == group_range[None, :]).astype(jnp.float32)
    terms = jnp.dot(
        band_residual, onehot, precision=lax.Precision.HIGHEST, preferred_element_type=jnp.float32
    )
    group_residual = lax.psum(terms, "band") * (NGROUPS / NB)
    return (ortho, band_residual, group_residual)


def solution(mesh):
    return jax.shard_map(
        local,
        mesh=mesh,
        in_specs=(P("band", "coef"), P("band", "coef"), P("coef"), P("band")),
        out_specs=(P("band", "coef"), P("band"), P()),
        check_vma=False,
    )
```

profile of v0, /device:TPU:0, one launch (start us, length us, event | category | flops | bytes accessed | tf_op | source)
XLA Modules:
  0.0 2639.6 jit_solution(11342121475017291769)
XLA Ops:
  7.2 33.4 %copy.17 = f32[128,65536]{0,1:T(8,128)} copy(f32[128,65536]{1,0:T(8,128)} %param.4) | data formatting | bytes 67108864 | tf_op args[0]
  40.6 31.1 %copy.18 = f32[128,8,8192]{2,0,1:T(8,128)} copy(f32[128,8,8192]{0,2,1:T(8,128)} %bitcast.156) | data formatting | bytes 67108864 | tf_op jit(solution)/shard_map/all_to_all | solution.py:11
  71.7 735.1 %all_to_all.38 = f32[128,8,8192]{2,0,1:T(8,128)} all-to-all(f32[128,8,8192]{2,0,1:T(8,128)} %copy.18), channel_id=1, replica_groups=mesh['band'=8,'coef'=4] {'band'}, dimensions={1} | all-to-all | bytes 67108864 | tf_op jit(solution)/shard_map/all_to_all | solution.py:11
  806.8 117.0 %fusion.74 = f32[1024,1024]{0,1:T(8,128)} fusion(f32[1024,8192]{1,0:T(8,128)} %bitcast.157), kind=kOutput, calls=%fused_computation.177 | convolution fusion | flops 103079215104 | bytes 37748736 | tf_op jit(solution)/shard_map/dot_general | solution.py:12
  923.9 141.9 %all-reduce.3.cloned.1.call-done = f32[1024,1024]{0,1:T(8,128)} async-done(((f32[1024,1024]{0,1:T(8,128)}), f32[1024,1024]{0,1:T(8,128)}) %all-reduce.3.cloned.1.call-update) | async-done | bytes 4194320 | tf_op jit(solution)/shard_map/psum | solution.py:15
  1105.7 11.9 cholesky.244
  1157.7 12.1 cholesky.487
  1285.6 23.2 while.1
  1308.8 79.0 %custom-call.69 = f32[8,128,128]{1,2,0:T(8,128)S(1)} custom-call(f32[8,128,128]{2,1,0:T(8,128)S(1)} %get-tuple-element.10), custom_call_target="InvertDiagBlocksLowerTriangular" | custom-call | tf_op jit(solution)/shard_map/triangular_solve | solution.py:17
  1387.8 12.6 constant_dynamic-update-slice_fusion.17
  1431.6 12.2 fusion.16
  1443.8 13.9 constant_dynamic-update-slice_fusion.14
  1457.7 14.1 fusion.19
  1471.8 12.5 constant_dynamic-update-slice_fusion.13
  1484.3 17.1 convolution_subtract_fusion.2
  1508.2 19.3 convolution_subtract_fusion.4
  1533.3 23.5 convolution_subtract_fusion.3
  1571.8 33.4 %copy.22 = f32[128,65536]{0,1:T(8,128)} copy(f32[128,65536]{1,0:T(8,128)} %param.5) | data formatting | bytes 67108864 | tf_op args[1]
  1605.4 687.3 %all-to-all-done.1 = f32[8,128,8192]{2,1,0:T(8,128)} async-done(((f32[8,128,8192]{2,1,0:T(8,128)}), f32[8,128,8192]{2,1,0:T(8,128)}, u32[]{:S(2)}, u32[]{:S(2)}) %all-to-all-start.1) | async-done | bytes 33554464 | tf_op jit(solution)/shard_map/all_to_all | solution.py:18
  2292.7 31.0 %copy.21 = f32[128,8,8192]{0,2,1:T(8,128)} copy(f32[128,8,8192]{2,0,1:T(8,128)} %bitcast.35) | data formatting | bytes 67108864 | tf_op jit(solution)/shard_map/all_to_all | solution.py:18
  2323.7 228.0 %gather_fusion = f32[65536,128]{1,0:T(8,128)} fusion(f32[128,65536]{0,1:T(8,128)} %bitcast.154, s32[65536]{0:T(1024)S(1)} %fusion.45), kind=kCustom, calls=%fused_computation | custom fusion | bytes 67371008 | tf_op jit(solution)/shard_map/jit(_take)/gather | solution.py:19
  2551.7 20.7 fusion.1
  2578.3 33.5 %copy.23 = f32[128,65536]{1,0:T(8,128)} copy(f32[128,65536]{0,1:T(8,128)} %bitcast.155) | data formatting | bytes 67108864
  2611.7 20.3 psum.23
  (110 shorter events, 279.2 us)
Async XLA Ops:
  7.2 1058.6 %all-reduce.3.cloned.1.call-start = ((), (), s32[]{:S(2)}) async-start(), calls=%async_computation.2 | async-start | bytes 8388608 | tf_op jit(solution)/shard_map/psum | solution.py:15
  1075.7 2.0 copy-start.3
  1400.4 31.3 %copy-start = (f32[128,8192]{1,0:T(8,128)}, f32[128,8192]{1,0:T(8,128)S(1)}, u32[]{:S(2)}) copy-start(f32[128,8192]{1,0:T(8,128)S(1)} %get-tuple-element.79) | copy-start | bytes 12582916
  1415.5 16.1 copy-start.1
  1431.6 12.2 copy-start.2
  1564.7 728.0 %all-to-all-start.1 = ((f32[8,128,8192]{2,1,0:T(8,128)}), f32[8,128,8192]{2,1,0:T(8,128)}, u32[]{:S(2)}, u32[]{:S(2)}) async-start(f32[8,128,8192]{2,1,0:T(8,128)} %bitcast.166), calls=%async_computation.1 | async-start | bytes 67108864 | tf_op jit(solution)/shard_map/all_to_all | solution.py:18
  1571.8 33.4 %copy-start.4 = (s32[65536]{0:T(1024)S(1)}, s32[65536]{0:T(1024)}, u32[]{:S(2)}) copy-start(s32[65536]{0:T(1024)} %param.6) | copy-start | bytes 786436
  2551.7 26.4 copy-start.5
  2578.1 33.7 %copy-start.6 = (f32[128]{0:T(128)}, f32[128]{0:T(128)S(1)}, u32[]{:S(2)}) copy-start(f32[128]{0:T(128)S(1)} %add_sqrt_fusion) | copy-start | bytes 1540
Sparse Core Ops, SparseCore 0:
  924.0 141.7 all-reduce.2
where the time goes:
time: 2650 us; the launch traced here: 2640 us
  waiting for transfers between devices  829 us (31%)
  blocking collectives  761 us (29%)
  local copies, waits for them, and re-layouts  424 us (16%)
  matrix products  317 us (12%)
  other arithmetic  282 us (11%)
    all_to_all x1, blocking collectives, local(): lax.all_to_all(coeffs, 'band', split_axis=1, concat_axis=0, tiled=True)  735 us
    all_to_all x1, waiting for transfers between devices, local(): lax.all_to_all(ortho_cols, 'band', split_axis=0, concat_axis=1, tiled=True)  687 us
    gather x1, local copies, waits for them, and re-layouts, local(): aligned = jnp.take(ortho, index_map, axis=1)  228 us
    another operation x15, matrix products, local(): lax.linalg.triangular_solve(factor, columns, left_side=True, lower=True)  177 us
    another operation x30, other arithmetic, local(): factor = jnp.linalg.cholesky(margin)  172 us
    psum x1, waiting for transfers between devices, local(): margin = lax.psum(partial_value, ('band', 'coef'))  142 us
    dot_general x1, matrix products, local(): jnp.dot(columns, columns.T, precision=lax.Precision.HIGHEST, preferred_el...  117 us
    unnamed x17, local copies, waits for them, and re-layouts  102 us
  transfers between devices with their start and end apart: 2, of which 2 were waited for; matrix products, arithmetic and copies ran while one was open for 1% of the time, Pallas kernels for 0%

commit v1 on v0

--- a/solution.py
+++ b/solution.py
@@ -12,7 +12,7 @@
     partial_value = jnp.dot(
         columns, columns.T, precision=lax.Precision.HIGHEST, preferred_element_type=jnp.float32
     )
-    margin = lax.psum(partial_value, ("band", "coef"))
+    margin = lax.psum(lax.psum(partial_value, "coef"), "band")
     factor = jnp.linalg.cholesky(margin)
     ortho_cols = lax.linalg.triangular_solve(factor, columns, left_side=True, lower=True)
     ortho = lax.all_to_all(ortho_cols, "band", split_axis=0, concat_axis=1, tiled=True)

time: 2650 us -> 2750 us (1.038)
  waiting for transfers between devices: 829 us -> 934 us
    psum x1 -> x2, waiting for transfers between devices: 142 us -> 245 us  [local(): margin = lax.psum(lax.psum(partial_value, 'coef'), 'band')]
  transfers between devices with their start and end apart: 2 -> 3, of which waited for: 2 -> 3; matrix products, arithmetic and copies ran while one was open for 1% -> 1% of each run, Pallas kernels for 0% -> 0%
where the time goes in v1:
time: 2750 us; the launch traced here: 2740 us
  waiting for transfers between devices  934 us (34%)
  blocking collectives  761 us (28%)
  local copies, waits for them, and re-layouts  424 us (15%)
  matrix products  317 us (12%)
  other arithmetic  282 us (10%)
    all_to_all x1, blocking collectives, local(): lax.all_to_all(coeffs, 'band', split_axis=1, concat_axis=0, tiled=True)  735 us
    all_to_all x1, waiting for transfers between devices, local(): lax.all_to_all(ortho_cols, 'band', split_axis=0, concat_axis=1, tiled=True)  689 us
    psum x2, waiting for transfers between devices, local(): margin = lax.psum(lax.psum(partial_value, 'coef'), 'band')  245 us
    gather x1, local copies, waits for them, and re-layouts, local(): aligned = jnp.take(ortho, index_map, axis=1)  228 us
    another operation x15, matrix products, local(): lax.linalg.triangular_solve(factor, columns, left_side=True, lower=True)  177 us
    another operation x30, other arithmetic, local(): factor = jnp.linalg.cholesky(margin)  172 us
    dot_general x1, matrix products, local(): jnp.dot(columns, columns.T, precision=lax.Precision.HIGHEST, preferred_el...  117 us
    unnamed x17, local copies, waits for them, and re-layouts  102 us
  transfers between devices with their start and end apart: 3, of which 3 were waited for; matrix products, arithmetic and copies ran while one was open for 1% of the time, Pallas kernels for 0%

profile of v1, /device:TPU:0, one launch (start us, length us, event | category | flops | bytes accessed | tf_op | source)
XLA Modules:
  0.0 2744.6 jit_solution(11511541795989000729)
XLA Ops:
  7.2 33.4 %copy.17 = f32[128,65536]{0,1:T(8,128)} copy(f32[128,65536]{1,0:T(8,128)} %param.4) | data formatting | bytes 67108864 | tf_op args[0]
  40.6 31.1 %copy.18 = f32[128,8,8192]{2,0,1:T(8,128)} copy(f32[128,8,8192]{0,2,1:T(8,128)} %bitcast.156) | data formatting | bytes 67108864 | tf_op jit(solution)/shard_map/all_to_all | solution.py:11
  71.7 735.1 %all_to_all.38 = f32[128,8,8192]{2,0,1:T(8,128)} all-to-all(f32[128,8,8192]{2,0,1:T(8,128)} %copy.18), channel_id=1, replica_groups=mesh['band'=8,'coef'=4] {'band'}, dimensions={1} | all-to-all | bytes 67108864 | tf_op jit(solution)/shard_map/all_to_all | solution.py:11
  806.8 117.0 %fusion.74 = f32[1024,1024]{0,1:T(8,128)} fusion(f32[1024,8192]{1,0:T(8,128)} %bitcast.157), kind=kOutput, calls=%fused_computation.177 | convolution fusion | flops 103079215104 | bytes 37748736 | tf_op jit(solution)/shard_map/dot_general | solution.py:12
  923.9 84.7 %all-reduce.4.cloned.1.call-done = f32[1024,1024]{0,1:T(8,128)} async-done(((f32[1024,1024]{0,1:T(8,128)}), f32[1024,1024]{0,1:T(8,128)}) %all-reduce.4.cloned.1.call-update) | async-done | bytes 4194320 | tf_op jit(solution)/shard_map/psum | solution.py:15
  1008.7 160.2 %all-reduce.6.cloned.1.call-done = f32[1024,1024]{0,1:T(8,128)} async-done(((f32[1024,1024]{0,1:T(8,128)}), f32[1024,1024]{0,1:T(8,128)}) %all-reduce.6.cloned.1.call-update) | async-done | bytes 4194320 | tf_op jit(solution)/shard_map/psum | solution.py:15
  1260.8 12.1 cholesky.487
  1388.7 23.2 while.1
  1411.9 79.0 %custom-call.69 = f32[8,128,128]{1,2,0:T(8,128)S(1)} custom-call(f32[8,128,128]{2,1,0:T(8,128)S(1)} %get-tuple-element.10), custom_call_target="InvertDiagBlocksLowerTriangular" | custom-call | tf_op jit(solution)/shard_map/triangular_solve | solution.py:17
  1490.9 12.6 constant_dynamic-update-slice_fusion.17
  1534.8 12.2 fusion.16
  1547.0 13.9 constant_dynamic-update-slice_fusion.14
  1560.8 14.1 fusion.19
  1574.9 12.5 constant_dynamic-update-slice_fusion.13
  1587.4 17.1 convolution_subtract_fusion.2
  1611.3 19.3 convolution_subtract_fusion.4
  1636.4 23.5 convolution_subtract_fusion.3
  1674.9 33.4 %copy.22 = f32[128,65536]{0,1:T(8,128)} copy(f32[128,65536]{1,0:T(8,128)} %param.5) | data formatting | bytes 67108864 | tf_op args[1]
  1708.5 688.9 %all-to-all-done.1 = f32[8,128,8192]{2,1,0:T(8,128)} async-done(((f32[8,128,8192]{2,1,0:T(8,128)}), f32[8,128,8192]{2,1,0:T(8,128)}, u32[]{:S(2)}, u32[]{:S(2)}) %all-to-all-start.1) | async-done | bytes 33554464 | tf_op jit(solution)/shard_map/all_to_all | solution.py:18
  2397.4 31.0 %copy.21 = f32[128,8,8192]{0,2,1:T(8,128)} copy(f32[128,8,8192]{2,0,1:T(8,128)} %bitcast.35) | data formatting | bytes 67108864 | tf_op jit(solution)/shard_map/all_to_all | solution.py:18
  2428.4 228.0 %gather_fusion = f32[65536,128]{1,0:T(8,128)} fusion(f32[128,65536]{0,1:T(8,128)} %bitcast.154, s32[65536]{0:T(1024)S(1)} %fusion.45), kind=kCustom, calls=%fused_computation | custom fusion | bytes 67371008 | tf_op jit(solution)/shard_map/jit(_take)/gather | solution.py:19
  2656.4 20.7 fusion.1
  2682.9 33.5 %copy.23 = f32[128,65536]{1,0:T(8,128)} copy(f32[128,65536]{0,1:T(8,128)} %bitcast.155) | data formatting | bytes 67108864
  2716.4 20.6 psum.31
  (113 shorter events, 291.1 us)
Async XLA Ops:
  7.2 1001.5 %all-reduce.4.cloned.1.call-start = ((), (), s32[]{:S(2)}) async-start(), calls=%async_computation.2 | async-start | bytes 8388608 | tf_op jit(solution)/shard_map/psum | solution.py:15
  923.8 245.0 %all-reduce.6.cloned.1.call-start = ((), (), s32[]{:S(2)}) async-start(), calls=%async_computation.3 | async-start | bytes 8388608 | tf_op jit(solution)/shard_map/psum | solution.py:15
  1178.8 2.0 copy-start.3
  1503.5 31.3 %copy-start = (f32[128,8192]{1,0:T(8,128)}, f32[128,8192]{1,0:T(8,128)S(1)}, u32[]{:S(2)}) copy-start(f32[128,8192]{1,0:T(8,128)S(1)} %get-tuple-element.79) | copy-start | bytes 12582916
  1518.6 16.1 copy-start.1
  1534.7 12.2 copy-start.2
  1667.9 729.5 %all-to-all-start.1 = ((f32[8,128,8192]{2,1,0:T(8,128)}), f32[8,128,8192]{2,1,0:T(8,128)}, u32[]{:S(2)}, u32[]{:S(2)}) async-start(f32[8,128,8192]{2,1,0:T(8,128)} %bitcast.166), calls=%async_computation.1 | async-start | bytes 67108864 | tf_op jit(solution)/shard_map/all_to_all | solution.py:18
  1674.9 33.4 %copy-start.4 = (s32[65536]{0:T(1024)S(1)}, s32[65536]{0:T(1024)}, u32[]{:S(2)}) copy-start(s32[65536]{0:T(1024)} %param.6) | copy-start | bytes 786436
  2656.4 26.4 copy-start.5
  2682.7 33.7 %copy-start.6 = (f32[128]{0:T(128)}, f32[128]{0:T(128)S(1)}, u32[]{:S(2)}) copy-start(f32[128]{0:T(128)S(1)} %add_sqrt_fusion) | copy-start | bytes 1540
Sparse Core Ops, SparseCore 0:
  924.0 84.6 all-reduce.3
  1012.3 156.5 all-reduce.5
